TPU v7x, 32 devices: a whole 2x2x4 slice. The times are simulated.
32 devices in a mesh: elec: 4 (over y, core), pix: 8 (over z, x).
Axes of the slice: x: 2, y: 2, z: 4, core: 2. Of those that a mesh axis runs over, the one named last changes fastest.
Arguments:
- wavefronts: bfloat16 [1536, 2, 320, 256], P('elec', None, 'pix'), may hold values from -40 to 40, as said below
- trial_modes: float32 [2, 32, 320, 256], P(None, None, 'pix'), may hold values from -6 to 6
Outputs:
- sample_modes: float32 [2, 32, 320, 256], P(None, 'elec', None, 'pix')
Inputs may be any that keep to these rules, and one draw needn't show every extreme that they name: `wavefronts`: field samples of each electron's wavefront.
All inputs are finite; a program needn't handle non-finite values.
Results may differ from a plain program's by a relative error of at most 0.0075.
Values may be sent and summed in bfloat16 or wider, within the bound.
A program may use at most 128 MiB of HBM per device.

v0:
```python
import functools
import math

import jax
import jax.numpy as jnp
import numpy as np
from jax import lax
from jax.experimental import pallas as pl
from jax.experimental.pallas import tpu as pltpu
from jax.sharding import PartitionSpec as P

NS_STEPS = 8

HIGH = lax.Precision.HIGHEST
MESH = pl.DeviceIdType.MESH


def greet(*groups):
    barrier = pltpu.get_barrier_semaphore()
    for axis, peers in groups:
        for peer in peers:
            pl.semaphore_signal(barrier, inc=1, device_id={axis: peer}, device_id_type=MESH)
    return sum(len(peers) for _, peers in groups)


def remote(src, dst, send_sem, recv_sem, axis, peer):
    return pltpu.make_async_remote_copy(
        src_ref=src,
        dst_ref=dst,
        send_sem=send_sem,
        recv_sem=recv_sem,
        device_id={axis: peer},
        device_id_type=MESH,
    )


NT = (((1,), (1,)), ((), ()))
NN = (((1,), (0,)), ((), ()))


def dot(left, right, dims):
    return lax.dot_general(left, right, dims, preferred_element_type=jnp.float32)


def scatter_gather(n, peers, x_ref, held, out_ref, send_a, recv_a, send_b, recv_b):
    me = lax.axis_index("pix")
    started = []
    scatter = []
    for d in range(1, n):
        peer = peers[d - 1]
        copy = remote(x_ref.at[peer], held.at[d], send_a.at[d], recv_a.at[d], "pix", peer)
        copy.start()
        scatter.append(copy)
    total = x_ref[me]
    for d in range(1, n):
        scatter[d - 1].wait_recv()
        total = total + held[d]
    out_ref[me] = total
    for d in range(1, n):
        copy = remote(
            out_ref.at[me], out_ref.at[me], send_b.at[d], recv_b.at[d], "pix", peers[d - 1]
        )
        copy.start()
        started.append(copy)
    for d in range(1, n):
        source = lax.rem(me + n - d, n)
        block = out_ref.at[source]
        remote(block, block, send_b.at[d], recv_b.at[d], "pix", source).wait_recv()
    return scatter + started


def core_kernel(
    np_, ne, pieces, sub, electrons, modes,
    waves_ref, low_ref, chirp_ref, table_ref,
    out_ref,
    applied_ref, turn_ref, part_ref, lines_ref, launch_ref, spec_ref, send_ref, rows_a, both_ref, cut_ref, emb_ref,
    held_a, total_a, pay_ref, held_b, total_b,
    x_ref, pair, half, far, first_ref, gram_in,
    ps, es, gs,
):
    share = modes // ne
    rows, cols = chirp_ref.shape[1], chirp_ref.shape[2]
    pixels = waves_ref.shape[1] // 2
    order = 2 * modes
    chunk = order // ne
    depth = order // np_
    width = pixels // pieces
    me_p = lax.axis_index("pix")
    peers = [lax.rem(me_p + d, np_) for d in range(1, np_)]
    me = lax.axis_index("elec")
    core = lax.rem(me, 2)
    chip = me // 2
    chips = ne // 2
    partner = chip * 2 + 1 - core
    others = [lax.rem(chip + d, chips) for d in range(1, chips)]
    seats = [other * 2 + core for other in others]
    sources = [lax.rem(chip + chips - d, chips) for d in range(1, chips)]
    greeted = greet(("pix", peers), ("elec", [partner] + seats))
    rows_a[...] = jnp.zeros_like(rows_a)

    def correlate(fields, start):
        swapped = jnp.concatenate([-fields[modes:], fields[:modes]], axis=0)
        rows_a[:, 0:electrons] += dot(fields, waves_ref[:, pl.ds(start, sub)], NT) + dot(
            swapped, waves_ref[:, pl.ds(pl.multiple_of(pixels + start, 128), sub)], NT
        )

    def opening(step, carry):
        start = pl.multiple_of(step * sub, 128)
        correlate(low_ref[:, pl.ds(start, sub)], start)
        return carry

    lax.fori_loop(0, pixels // sub, opening, 0)
    for j in range(np_):
        part_ref[j] = rows_a[pl.ds(j * depth, depth), 0:electrons]
    pl.semaphore_wait(pltpu.get_barrier_semaphore(), greeted)
    started = scatter_gather(
        np_, peers, part_ref, held_a, total_a, ps.at[0], ps.at[1], ps.at[2], ps.at[3]
    )
    for j in range(np_):
        rows_a[pl.ds(j * depth, depth), 0:electrons] = total_a[j]

    def split_rows(value):
        upper = value.astype(jnp.bfloat16)
        both_ref[0:order, :] = upper
        both_ref[order : 2 * order, :] = (value - upper.astype(jnp.float32)).astype(jnp.bfloat16)

    def part(ref, lead, piece):
        return ref.at[lead, :, pl.ds(piece * width, width)]

    def cut(piece):
        return pl.ds(piece * width, width)

    def round_trip(turn, gathered, finish, beside):
        sa, ra, sb, rb, sc, rc, sd, rd, se, re = [es.at[10 * turn + i] for i in range(10)]
        first, second = {}, {}

        def compute(piece):
            def body(step, carry):
                start = pl.multiple_of(piece * width + step * sub, 128)
                both = both_ref[...]
                from_re = dot(both, waves_ref[:, pl.ds(start, sub)], NN)
                from_im = dot(both, waves_ref[:, pl.ds(pl.multiple_of(pixels + start, 128), sub)], NN)
                from_re = from_re[:order] + from_re[order:]
                from_im = from_im[:order] + from_im[order:]
                real = from_re[:modes] + from_im[modes:]
                imag = from_re[modes:] - from_im[:modes]
                if chunk % 16 == 0:
                    whole = jnp.concatenate([real, imag], axis=0).astype(jnp.bfloat16)
                    for j in range(ne):
                        x_ref[turn, j, :, pl.ds(start, sub)] = whole[j * chunk : (j + 1) * chunk]
                else:
                    cut_ref[0:modes, :] = real
                    cut_ref[modes:order, :] = imag
                    for j in range(ne):
                        x_ref[turn, j, :, pl.ds(start, sub)] = cut_ref[
                            pl.ds(j * chunk, chunk), :
                        ].astype(jnp.bfloat16)
                return carry

            lax.fori_loop(0, width // sub, body, 0)
            for d, other in enumerate(others + [chip]):
                slot = d * pieces + piece
                copy = remote(
                    part(x_ref.at[turn], other * 2 + 1 - core, piece),
                    part(pair.at[turn], d, piece),
                    sa.at[slot], ra.at[slot], "elec", partner,
                )
                copy.start()
                started.append(copy)
                first[d, piece] = copy

        def cross(piece):
            for d in range(chips - 1):
                slot = d * pieces + piece
                first[d, piece].wait_recv()
                half[turn, d, :, cut(piece)] = (
                    x_ref[turn, seats[d], :, cut(piece)].astype(jnp.float32)
                    + pair[turn, d, :, cut(piece)].astype(jnp.float32)
                ).astype(jnp.bfloat16)
                copy = remote(
                    part(half.at[turn], d, piece), part(far.at[turn], d, piece),
                    sb.at[slot], rb.at[slot], "elec", seats[d],
                )
                copy.start()
                started.append(copy)
                second[d, piece] = copy

        def close(piece):
            first[chips - 1, piece].wait_recv()
            total = x_ref[turn, me, :, cut(piece)].astype(jnp.float32) + pair[
                turn, chips - 1, :, cut(piece)
            ].astype(jnp.float32)
            for d in range(chips - 1):
                second[d, piece].wait_recv()
                total = total + far[turn, d, :, cut(piece)].astype(jnp.float32)
            gathered[me, :, cut(piece)] = total.astype(jnp.bfloat16)
            block = part(gathered, me, piece)
            for d in range(chips - 1):
                slot = d * pieces + piece
                copy = remote(block, block, sc.at[slot], rc.at[slot], "elec", seats[d])
                copy.start()
                started.append(copy)
            copy = remote(block, block, sd.at[piece], rd.at[piece], "elec", partner)
            copy.start()
            started.append(copy)

        def relay(piece):
            for d in range(chips - 1):
                slot = d * pieces + piece
                source = sources[d] * 2 + core
                block = part(gathered, source, piece)
                remote(block, block, sc.at[slot], rc.at[slot], "elec", source).wait_recv()
                copy = remote(block, block, se.at[slot], re.at[slot], "elec", partner)
                copy.start()
                started.append(copy)

        def arrive(piece):
            block = part(gathered, partner, piece)
            remote(block, block, sd.at[piece], rd.at[piece], "elec", partner).wait_recv()
            for d in range(chips - 1):
                slot = d * pieces + piece
                block = part(gathered, sources[d] * 2 + 1 - core, piece)
                remote(block, block, se.at[slot], re.at[slot], "elec", partner).wait_recv()
            finish(piece)

        for tick in range(pieces + 5):
            for lag, stage in ((0, compute), (1, cross), (3, close), (4, relay), (5, arrive)):
                if 0 <= tick - lag < pieces:
                    stage(tick - lag)
            if tick == pieces:
                beside()

    def stacked(gathered, start):
        if chunk % 16 == 0:
            return jnp.concatenate([gathered[j, :, pl.ds(start, sub)] for j in range(ne)], axis=0)
        for j in range(ne):
            cut_ref[pl.ds(j * chunk, chunk), :] = gathered[j, :, pl.ds(start, sub)].astype(
                jnp.float32
            )
        return cut_ref[...].astype(jnp.bfloat16)

    split_rows(rows_a[:, 0:electrons])
    rows_a[...] = jnp.zeros_like(rows_a)

    def project_piece(piece):
        def body(step, carry):
            start = pl.multiple_of(piece * width + step * sub, 128)
            fields = stacked(first_ref, start)
            correlate(fields, start)
            rows_a[:, electrons : electrons + order] += dot(fields, fields, NT)
            return carry

        lax.fori_loop(0, width // sub, body, 0)

    round_trip(0, first_ref, project_piece, lambda: None)
    for j in range(np_):
        pay_ref[j] = rows_a[pl.ds(j * depth, depth), :]
    started += scatter_gather(
        np_, peers, pay_ref, held_b, total_b, ps.at[4], ps.at[5], ps.at[6], ps.at[7]
    )
    for j in range(np_):
        rows_a[pl.ds(j * depth, depth), :] = total_b[j]

    row_id = lax.broadcasted_iota(jnp.int32, (order, order), 0)
    col_id = lax.broadcasted_iota(jnp.int32, (order, order), 1)
    raw = rows_a[:, electrons : electrons + order]
    trace = 2.0 * jnp.sum(
        jnp.sum(jnp.where(row_id == col_id, raw, 0.0), axis=1, keepdims=True), axis=0, keepdims=True
    )
    split_rows(rows_a[:, 0:electrons] / jnp.sqrt(trace))

    def first_turn():
        gram_re = raw[:modes, :modes] + raw[modes:, modes:]
        gram_im = raw[:modes, modes:] - raw[modes:, :modes]
        emb_ref[0:modes, 0:modes] = gram_re
        emb_ref[0:modes, modes:order] = -gram_im
        emb_ref[modes:order, 0:modes] = gram_im
        emb_ref[modes:order, modes:order] = gram_re
        identity = jnp.where(row_id == col_id, 1.0, 0.0).astype(jnp.float32)
        turn_ref[...] = newton_schulz(emb_ref[...] / trace, identity)

    emb2 = [jnp.zeros((order, order), jnp.float32)]

    def gram_piece(piece):
        def body(step, carry):
            fields = stacked(applied_ref, pl.multiple_of(piece * width + step * sub, 128))
            return carry + dot(fields, fields, NT)

        emb2[0] = lax.fori_loop(0, width // sub, body, emb2[0])

    round_trip(1, applied_ref, gram_piece, first_turn)
    raw2 = emb2[0]
    gram_re = raw2[:modes, :modes] + raw2[modes:, modes:]
    gram_im = raw2[:modes, modes:] - raw2[modes:, :modes]
    low = modes // 2
    emb_ref[0:modes, 0:modes] = gram_re
    emb_ref[0:modes, modes:order] = gram_im
    gram_in[0, :, 0:order] = emb_ref[0:low, 0:order]
    gram_in[0, :, order : 2 * order] = emb_ref[low:modes, 0:order]
    last = []
    for d in range(1, np_):
        copy = remote(
            gram_in.at[0], gram_in.at[d], gs.at[0, d], gs.at[1, d], "pix", peers[d - 1]
        )
        copy.start()
        last.append(copy)
    total = gram_in[0]
    for d in range(1, np_):
        last[d - 1].wait_recv()
        total = total + gram_in[d]
    emb_ref[0:low, 0:order] = total[:, 0:order]
    emb_ref[low:modes, 0:order] = total[:, order : 2 * order]
    gram_re = emb_ref[0:modes, 0:modes]
    gram_im = emb_ref[0:modes, modes:order]
    emb_ref[0:modes, modes:order] = gram_im
    emb_ref[modes:order, 0:modes] = -gram_im
    emb_ref[modes:order, modes:order] = gram_re
    first_root = turn_ref[...]
    first_t = first_root.T
    raw = 0.5 * jnp.dot(
        jnp.dot(first_t, emb_ref[...], precision=HIGH), first_root, precision=HIGH
    )
    gram_re = raw[:modes, :modes] + raw[modes:, modes:]
    gram_im = raw[:modes, modes:] - raw[modes:, :modes]
    emb_ref[0:modes, 0:modes] = gram_re
    emb_ref[0:modes, modes:order] = -gram_im
    emb_ref[modes:order, 0:modes] = gram_im
    emb_ref[modes:order, modes:order] = gram_re
    embedded = emb_ref[...]
    diagonal = row_id == col_id
    trace = jnp.sum(
        jnp.sum(jnp.where(diagonal, embedded, 0.0), axis=1, keepdims=True), axis=0, keepdims=True
    )
    identity = jnp.where(diagonal, 1.0, 0.0).astype(jnp.float32)
    second_root = newton_schulz(embedded / trace, identity) / jnp.sqrt(trace)
    turn_ref[...] = jnp.dot(second_root.T, first_t, precision=HIGH)
    for part_of in range(2):
        emb_ref[pl.ds(part_of * share, share), :] = turn_ref[
            pl.ds(part_of * modes + me * share, share), :
        ]
    mine = emb_ref[0 : 2 * share, :]
    upper = mine.astype(jnp.bfloat16)
    lower = (mine - upper.astype(jnp.float32)).astype(jnp.bfloat16)
    group = next(count for count in (8, 5, 4, 2, 1) if rows % count == 0)

    def rotate(step, carry):
        start = pl.multiple_of(step * (group * cols), 128)
        if chunk % 16 == 0:
            fields = jnp.concatenate(
                [applied_ref[j, :, pl.ds(start, group * cols)] for j in range(ne)], axis=0
            )
        else:
            fields = jnp.concatenate(
                [
                    applied_ref[j, :, pl.ds(start, group * cols)].astype(jnp.float32)
                    for j in range(ne)
                ],
                axis=0,
            ).astype(jnp.bfloat16)
        turned = dot(upper, fields, NN) + dot(lower, fields, NN)
        for i in range(group):
            for b in range(cols // 128):
                lines_ref[b, pl.ds((step * group + i) * 2 * share, 2 * share), :] = turned[
                    :, i * cols + b * 128 : i * cols + (b + 1) * 128
                ]
        return carry

    lax.fori_loop(0, rows // group, rotate, 0)
    chirp_re, chirp_im = chirp_ref[0], chirp_ref[1]
    for m in range(share):
        real = jnp.concatenate(
            [lines_ref[b, pl.ds(m, rows, stride=2 * share), :] for b in range(cols // 128)], axis=1
        )
        imag = jnp.concatenate(
            [
                lines_ref[b, pl.ds(share + m, rows, stride=2 * share), :]
                for b in range(cols // 128)
            ],
            axis=1,
        )
        launch_ref[m * rows : (m + 1) * rows, 0:cols] = chirp_re * real - chirp_im * imag
        launch_ref[m * rows : (m + 1) * rows, cols : 2 * cols] = chirp_re * imag + chirp_im * real
    launch = launch_ref[...]
    upper = launch.astype(jnp.bfloat16)
    lower = (launch - upper.astype(jnp.float32)).astype(jnp.bfloat16)
    spec_ref[...] = (
        dot(upper, table_ref[0], NN) + dot(upper, table_ref[1], NN) + dot(lower, table_ref[0], NN)
    )
    thin = cols // np_
    for p in range(np_):
        for c in range(2):
            for m in range(share):
                at = (2 * p + c) * thin
                to = (c * share + m) * thin
                send_ref[p, :, to : to + thin] = spec_ref[
                    m * rows : (m + 1) * rows, at : at + thin
                ].astype(jnp.bfloat16)
    swaps = []
    for d in range(1, np_):
        copy = remote(
            send_ref.at[peers[d - 1]], out_ref.at[me_p], gs.at[2, d], gs.at[3, d], "pix",
            peers[d - 1],
        )
        copy.start()
        swaps.append(copy)
    out_ref[me_p] = send_ref[me_p]
    for d in range(1, np_):
        source = lax.rem(me_p + np_ - d, np_)
        block = out_ref.at[source]
        remote(block, block, gs.at[2, d], gs.at[3, d], "pix", source).wait_recv()
    for copy in started + last + swaps:
        copy.wait_send()


def middle(waves, low, chirp, tables, mode_count):
    np_ = lax.axis_size("pix")
    ne = lax.axis_size("elec")
    electrons = waves.shape[0]
    pixels = waves.shape[1] // 2
    order = 2 * mode_count
    chunk = order // ne
    depth = order // np_
    pieces = next(count for count in (4, 2, 1) if pixels % (128 * count) == 0)
    sub = next(size for size in (1280, 640, 512, 256, 128) if pixels // pieces % size == 0)
    chips = ne // 2
    wide = electrons + order + -order % 128
    share = mode_count // ne
    rows, cols = chirp.shape[1:]
    lanes = 2 * share * (cols // np_)
    vmem = pl.BlockSpec(memory_space=pltpu.VMEM)
    dma = pltpu.SemaphoreType.DMA
    f32, bf16 = jnp.float32, jnp.bfloat16
    return pl.pallas_call(
        functools.partial(core_kernel, np_, ne, pieces, sub, electrons, mode_count),
        out_shape=jax.ShapeDtypeStruct((np_, rows, lanes), bf16),
        in_specs=[vmem] * 4,
        out_specs=vmem,
        scratch_shapes=[
            pltpu.VMEM((ne, chunk, pixels), bf16),
            pltpu.VMEM((order, order), f32),
            pltpu.VMEM((np_, depth, electrons), f32),
            pltpu.VMEM((cols // 128, rows * 2 * share, 128), f32),
            pltpu.VMEM((share * rows, 2 * cols), f32),
            pltpu.VMEM((share * rows, 2 * cols), f32),
            pltpu.VMEM((np_, rows, lanes), bf16),
            pltpu.VMEM((order, wide), f32),
            pltpu.VMEM((2 * order, electrons), bf16),
            pltpu.VMEM((order, sub), f32),
            pltpu.VMEM((order, order), f32),
            pltpu.VMEM((np_, depth, electrons), f32),
            pltpu.VMEM((np_, depth, electrons), f32),
            pltpu.VMEM((np_, depth, wide), f32),
            pltpu.VMEM((np_, depth, wide), f32),
            pltpu.VMEM((np_, depth, wide), f32),
            pltpu.VMEM((2, ne, chunk, pixels), bf16),
            pltpu.VMEM((2, chips, chunk, pixels), bf16),
            pltpu.VMEM((2, chips, chunk, pixels), bf16),
            pltpu.VMEM((2, chips, chunk, pixels), bf16),
            pltpu.VMEM((ne, chunk, pixels), bf16),
            pltpu.VMEM((np_, mode_count // 2, 2 * order), f32),
            dma((8, np_)),
            dma((20, chips * pieces)),
            dma((4, np_)),
        ],
        compiler_params=pltpu.CompilerParams(
            collective_id=1, has_side_effects=True, vmem_limit_bytes=60 * 1024 * 1024
        ),
        name="middle",
    )(waves, low, chirp, tables)


def newton_schulz(scaled, identity):
    inverse_root = identity
    for step in range(NS_STEPS):
        product = scaled if step == 0 else jnp.dot(inverse_root, scaled, precision=HIGH)
        correction = 1.5 * identity - 0.5 * product
        if step == 0:
            inverse_root = correction
        else:
            inverse_root = jnp.dot(correction, inverse_root, precision=HIGH)
        if step + 1 < NS_STEPS:
            scaled = jnp.dot(scaled, correction, precision=HIGH)
    return inverse_root


def dft_table(length):
    index = np.arange(length, dtype=np.int64)
    angle = 2.0 * np.pi / length * (index[:, None] * index[None, :] % length)
    return np.cos(angle).astype(np.float32), -np.sin(angle).astype(np.float32)


def split(table):
    upper = table.astype(jnp.bfloat16)
    lower = (table - upper.astype(np.float32)).astype(jnp.bfloat16)
    return upper, lower


def chirp_phase(row_pos, col_pos, row_total, col_total, factor):
    row_term = (row_pos - row_total / 2.0) ** 2 / row_total
    col_term = (col_pos - col_total / 2.0) ** 2 / col_total
    angle = math.pi * factor * (row_term[:, None] + col_term[None, :])
    return (jnp.cos(angle), jnp.sin(angle))


def column_tables(length, pix_count):
    table_re, table_im = dft_table(length)
    full = np.stack([np.stack([table_re, table_im], 1), np.stack([-table_im, table_re], 1)])
    full = full.reshape(2, length, 2, pix_count, length // pix_count).transpose(0, 1, 3, 2, 4)
    return np.stack(split(full.reshape(2 * length, 2 * length)))


def row_section(spectrum, share, col_pos, row_total, col_total):
    width = col_pos.shape[0]
    table_re, table_im = dft_table(row_total)
    upper, lower = split(np.concatenate([table_re, table_im], axis=0))
    tables = np.concatenate([upper, lower], axis=0)
    wide = jnp.dot(jnp.asarray(tables), spectrum, preferred_element_type=jnp.float32)
    wide = wide[: 2 * row_total] + wide[2 * row_total :]
    half = share * width
    out_re = wide[:row_total, :half] - wide[row_total:, half:]
    out_im = wide[:row_total, half:] + wide[row_total:, :half]
    row_pos = jnp.arange(row_total, dtype=jnp.float32)
    chirp_re, chirp_im = chirp_phase(row_pos, col_pos, row_total, col_total, 0.25)
    out_re = out_re.reshape(row_total, share, width).transpose(1, 0, 2)
    out_im = out_im.reshape(row_total, share, width).transpose(1, 0, 2)
    return jnp.stack([chirp_re * out_re - chirp_im * out_im, chirp_re * out_im + chirp_im * out_re])


def shards(wavefronts, trial_modes):
    electrons_dev, _, rows_dev, cols = wavefronts.shape
    mode_count = trial_modes.shape[1]
    order = 2 * mode_count
    pixels = rows_dev * cols
    groups = lax.axis_size("elec")
    share = mode_count // groups
    waves = wavefronts.reshape(electrons_dev, 2 * pixels)
    low = trial_modes.astype(jnp.bfloat16).reshape(order, pixels)

    pix_count = lax.axis_size("pix")
    row_total = rows_dev * pix_count
    row_pos = (lax.axis_index("pix") * rows_dev + jnp.arange(rows_dev, dtype=jnp.int32)).astype(
        jnp.float32
    )
    chirp = jnp.stack(
        chirp_phase(row_pos, jnp.arange(cols, dtype=jnp.float32), row_total, cols, 0.5)
    )
    tables = jnp.asarray(column_tables(cols, pix_count))
    column_block = middle(waves, low, chirp, tables, mode_count).reshape(row_total, -1)
    width = cols // pix_count
    col_pos = (lax.axis_index("pix") * width + jnp.arange(width, dtype=jnp.int32)).astype(
        jnp.float32
    )
    return row_section(column_block, share, col_pos, row_total, cols)


def solution(mesh):
    in_specs = (P("elec", None, "pix", None), P(None, None, "pix", None))
    out_specs = P(None, "elec", None, "pix")
    return jax.shard_map(shards, mesh=mesh, in_specs=in_specs, out_specs=out_specs, check_vma=False)
```

profile of v0, /device:TPU:0, one launch (start us, length us, event | category | flops | bytes accessed | tf_op | source)
XLA Modules:
  0.0 121.3 jit_solution(15609195082417405269)
XLA Ops:
  0.0 0.2 fusion.3
  0.3 0.6 pad_maximum_fusion.1.chirp_ref
  0.9 0.3 fusion.1
  1.2 1.9 %convert_element_type.18 = bf16[2,32,40,256]{3,2,1,0:T(8,128)(2,1)S(1)} convert(f32[2,32,40,256]{3,2,1,0:T(8,128)} %param.5) | non-fusion elementwise | flops 655360 | bytes 3932160 | tf_op jit(solution)/shard_map/convert_element_type | solution.py:537
  3.0 1.3 %copy.12 = bf16[8,8,40,256]{3,1,2,0:T(8,128)(2,1)} copy(bf16[8,8,40,256]{3,2,1,0:T(8,128)(2,1)S(1)} %bitcast.21) | data formatting | bytes 2621440
  4.4 15.2 %copy.11 = bf16[48,8,80,256]{3,1,2,0:T(8,128)(2,1)} copy(bf16[48,8,80,256]{3,2,1,0:T(8,128)(2,1)} %bitcast.20) | data formatting | bytes 31457280
  19.6 0.0 copy-start
  19.6 98.1 %middle.1 = bf16[8,40,512]{2,1,0:T(8,128)(2,1)} custom-call(bf16[384,20480]{1,0:T(8,128)(2,1)} %bitcast.19, bf16[64,10240]{1,0:T(8,128)(2,1)} %bitcast.22, f32[2,40,256]{2,1,0:T(8,128)} %pad_maximum_fusion.1.chirp_ref, bf16[2,512,512]{2,1,0:T(8,128)(2,1)} %constant.36.clone.table_ref), custom_call_target="tpu_custom_call" | custom-call | tf_op jit(solution)/shard_map/middle/pallas_call | solution.py:433
  117.7 0.0 copy-done
  117.7 1.8 %fusion.4 = f32[1280,512]{1,0:T(8,128)S(1)} fusion(bf16[1280,320]{1,0:T(8,128)(2,1)S(1)} %copy-done, bf16[320,512]{1,0:T(8,128)(2,1)} %bitcast.25), kind=kOutput, calls=%fused_computation.17 | convolution fusion | flops 419430400 | bytes 3768320 | tf_op jit(solution)/shard_map/dot_general | solution.py:517
  119.5 0.3 slice_add_fusion
  119.8 0.1 slice_add_fusion.1
  119.9 0.2 copy.10
  120.1 0.2 copy.9
  120.2 0.1 subtract_bitcast_fusion
  120.3 0.9 pad_maximum_fusion
  (4 shorter events, 0.0 us)
Async XLA Ops:
  19.6 98.1 %copy-start = (bf16[1280,320]{1,0:T(8,128)(2,1)S(1)}, bf16[1280,320]{1,0:T(8,128)(2,1)}, u32[]{:S(2)}) copy-start(bf16[1280,320]{1,0:T(8,128)(2,1)} %constant.37.clone) | copy-start | bytes 2457604
where the time goes:
time: 122 us; the launch traced here: 121 us
  Pallas kernels  98.1 us (80%)
  local copies, waits for them, and re-layouts  16.9 us (14%)
  other arithmetic  4.43 us (4%)
  matrix products  1.81 us (1%)
    pallas_call x1, Pallas kernels, middle(): pl.pallas_call(functools.partial(core_kernel, np_, ne, pieces, sub, elect...  98.1 us
    unnamed x4, local copies, waits for them, and re-layouts  16.6 us

commit v1 on v0

--- a/solution.py
+++ b/solution.py
@@ -13,6 +13,7 @@
 
 HIGH = lax.Precision.HIGHEST
 MESH = pl.DeviceIdType.MESH
+EBLOCK = 128
 
 
 def greet(*groups):
@@ -70,17 +71,19 @@
 
 
 def core_kernel(
-    np_, ne, pieces, sub, electrons, modes,
-    waves_ref, low_ref, chirp_ref, table_ref,
+    np_, ne, pieces, sub, electrons, modes, raw,
+    waves_hbm, trial_hbm, chirp_hbm, table_hbm,
     out_ref,
+    stage_ref, waves_ref, trial_ref, low_ref, chirp_ref, table_ref, pick_ref,
     applied_ref, turn_ref, part_ref, lines_ref, launch_ref, spec_ref, send_ref, rows_a, both_ref, cut_ref, emb_ref,
     held_a, total_a, pay_ref, held_b, total_b,
     x_ref, pair, half, far, first_ref, gram_in,
-    ps, es, gs,
+    ps, es, gs, load_sem,
 ):
     share = modes // ne
-    rows, cols = chirp_ref.shape[1], chirp_ref.shape[2]
-    pixels = waves_ref.shape[1] // 2
+    rows, cols = chirp_ref.shape[1:]
+    pixels = rows * cols
+    lines = sub // cols
     order = 2 * modes
     chunk = order // ne
     depth = order // np_
@@ -98,18 +101,107 @@
     greeted = greet(("pix", peers), ("elec", [partner] + seats))
     rows_a[...] = jnp.zeros_like(rows_a)
 
-    def correlate(fields, start):
+    def load(src, dst, slot):
+        copy = pltpu.make_async_copy(src, dst, load_sem.at[slot])
+        copy.start()
+        return copy
+
+    panels = cols // 128
+    trial_copies = [
+        load(trial_hbm.at[:, pl.ds(b * 128, 128)], trial_ref.at[b], 2 + b) for b in range(panels)
+    ]
+    if raw:
+        band, batch = 8, EBLOCK
+        blocks = electrons // batch
+
+        def wave_copy(step):
+            block, half_of = step // 2, lax.rem(step, 2)
+            at = (pl.ds(pl.multiple_of(block * batch, batch), batch), half_of)
+            return pltpu.make_async_copy(
+                waves_hbm.at[at], stage_ref.at[at], load_sem.at[2 + panels + step]
+            )
+
+        for step in range(2 * blocks):
+            wave_copy(step).start()
+    else:
+        wave_copy = load(waves_hbm, waves_ref, 2 + panels)
+    late_copies = [
+        load(chirp_hbm.at[:, me_p], chirp_ref, 0),
+        load(table_hbm, table_ref, 1),
+    ]
+    for copy in trial_copies:
+        copy.wait()
+
+    def lower_modes(row, carry):
+        fields = jnp.concatenate(
+            [trial_ref[b, pl.ds(row, order, stride=rows), :] for b in range(panels)], axis=1
+        ).astype(jnp.bfloat16)
+        at = pl.ds(pl.multiple_of(row * cols, 128), cols)
+        low_ref[0, :, at] = fields
+        low_ref[1, :, at] = jnp.concatenate([-fields[modes:], fields[:modes]], axis=0)
+        return carry
+
+    lax.fori_loop(0, rows, lower_modes, 0)
+
+    def wave(half_of, row, count):
+        return jnp.concatenate([waves_ref[half_of * rows + row + i] for i in range(count)], axis=1)
+
+    def correlate(fields, row):
         swapped = jnp.concatenate([-fields[modes:], fields[:modes]], axis=0)
-        rows_a[:, 0:electrons] += dot(fields, waves_ref[:, pl.ds(start, sub)], NT) + dot(
-            swapped, waves_ref[:, pl.ds(pl.multiple_of(pixels + start, 128), sub)], NT
+        rows_a[:, 0:electrons] += dot(fields, wave(0, row, lines), NT) + dot(
+            swapped, wave(1, row, lines), NT
         )
 
-    def opening(step, carry):
-        start = pl.multiple_of(step * sub, 128)
-        correlate(low_ref[:, pl.ds(start, sub)], start)
-        return carry
-
-    lax.fori_loop(0, pixels // sub, opening, 0)
+    if raw:
+        tile = band * 32
+        pick_row = lax.broadcasted_iota(jnp.int32, (tile, tile), 0)
+        pick_col = lax.broadcasted_iota(jnp.int32, (tile, tile), 1)
+        pick_ref[...] = jnp.where(
+            pick_col == lax.rem(pick_row, 32) * band + pick_row // 32, 1.0, 0.0
+        ).astype(jnp.bfloat16)
+
+        def sort_block(step, carry):
+            wave_copy(step).wait()
+            block, half_of = step // 2, lax.rem(step, 2)
+            base = pl.multiple_of(block * batch, batch)
+
+            def sort_band(band_of, carry):
+                sorted_tiles = []
+                for t in range(batch // 32):
+                    mixed = stage_ref[pl.ds(base + t * 32, 32), half_of, band_of]
+                    sorted_tiles.append(
+                        dot(pick_ref[...], mixed.reshape(tile, cols), NN).astype(jnp.bfloat16)
+                    )
+                by_row = []
+                for r in range(band):
+                    row_wave = jnp.concatenate(
+                        [value[r * 32 : (r + 1) * 32] for value in sorted_tiles], axis=0
+                    )
+                    waves_ref[half_of * rows + band_of * band + r, pl.ds(base, batch), :] = row_wave
+                    by_row.append(row_wave)
+                fields = low_ref[
+                    half_of, :, pl.ds(pl.multiple_of(band_of * band * cols, 128), band * cols)
+                ]
+                rows_a[:, pl.ds(base, batch)] += dot(
+                    fields, jnp.concatenate(by_row, axis=1), NT
+                )
+                return carry
+
+            lax.fori_loop(0, rows // band, sort_band, 0)
+            return carry
+
+        lax.fori_loop(0, 2 * blocks, sort_block, 0)
+    else:
+        wave_copy.wait()
+
+        def opening(step, carry):
+            at = pl.ds(pl.multiple_of(step * sub, 128), sub)
+            correlate(low_ref[0, :, at], step * lines)
+            return carry
+
+        lax.fori_loop(0, rows // lines, opening, 0)
+    for copy in late_copies:
+        copy.wait()
     for j in range(np_):
         part_ref[j] = rows_a[pl.ds(j * depth, depth), 0:electrons]
     pl.semaphore_wait(pltpu.get_barrier_semaphore(), greeted)
@@ -137,9 +229,10 @@
         def compute(piece):
             def body(step, carry):
                 start = pl.multiple_of(piece * width + step * sub, 128)
+                row = (piece * (width // sub) + step) * lines
                 both = both_ref[...]
-                from_re = dot(both, waves_ref[:, pl.ds(start, sub)], NN)
-                from_im = dot(both, waves_ref[:, pl.ds(pl.multiple_of(pixels + start, 128), sub)], NN)
+                from_re = dot(both, wave(0, row, lines), NN)
+                from_im = dot(both, wave(1, row, lines), NN)
                 from_re = from_re[:order] + from_re[order:]
                 from_im = from_im[:order] + from_im[order:]
                 real = from_re[:modes] + from_im[modes:]
@@ -246,7 +339,7 @@
         def body(step, carry):
             start = pl.multiple_of(piece * width + step * sub, 128)
             fields = stacked(first_ref, start)
-            correlate(fields, start)
+            correlate(fields, (piece * (width // sub) + step) * lines)
             rows_a[:, electrons : electrons + order] += dot(fields, fields, NT)
             return carry
 
@@ -412,30 +505,47 @@
         copy.wait_send()
 
 
-def middle(waves, low, chirp, tables, mode_count):
+def middle(waves, trial, chirp, tables):
     np_ = lax.axis_size("pix")
     ne = lax.axis_size("elec")
-    electrons = waves.shape[0]
-    pixels = waves.shape[1] // 2
+    electrons, _, rows, cols = waves.shape
+    mode_count = trial.shape[1]
+    pixels = rows * cols
     order = 2 * mode_count
     chunk = order // ne
     depth = order // np_
-    pieces = next(count for count in (4, 2, 1) if pixels % (128 * count) == 0)
-    sub = next(size for size in (1280, 640, 512, 256, 128) if pixels // pieces % size == 0)
+    raw = rows % 8 == 0 and electrons % EBLOCK == 0
+    if raw:
+        waves = waves.reshape(electrons, 2, rows // 8, 8, cols)
+        stage = waves.shape
+    else:
+        waves = waves.transpose(1, 2, 0, 3).reshape(2 * rows, electrons, cols)
+        stage = (1, 1, 1, 8, 128)
+    trial = trial.reshape(order * rows, cols)
+    pieces = next(count for count in (4, 2, 1) if rows % count == 0)
+    lines = next(size for size in (5, 4, 2, 1) if rows // pieces % size == 0)
+    sub = lines * cols
     chips = ne // 2
     wide = electrons + order + -order % 128
     share = mode_count // ne
-    rows, cols = chirp.shape[1:]
     lanes = 2 * share * (cols // np_)
     vmem = pl.BlockSpec(memory_space=pltpu.VMEM)
+    hbm = pl.BlockSpec(memory_space=pl.ANY)
     dma = pltpu.SemaphoreType.DMA
     f32, bf16 = jnp.float32, jnp.bfloat16
     return pl.pallas_call(
-        functools.partial(core_kernel, np_, ne, pieces, sub, electrons, mode_count),
+        functools.partial(core_kernel, np_, ne, pieces, sub, electrons, mode_count, raw),
         out_shape=jax.ShapeDtypeStruct((np_, rows, lanes), bf16),
-        in_specs=[vmem] * 4,
+        in_specs=[hbm] * 4,
         out_specs=vmem,
         scratch_shapes=[
+            pltpu.VMEM(stage, bf16),
+            pltpu.VMEM((2 * rows, electrons, cols), bf16),
+            pltpu.VMEM((cols // 128, order * rows, 128), f32),
+            pltpu.VMEM((2, order, pixels), bf16),
+            pltpu.VMEM((2, rows, cols), f32),
+            pltpu.VMEM(tables.shape, bf16),
+            pltpu.VMEM((256, 256), bf16),
             pltpu.VMEM((ne, chunk, pixels), bf16),
             pltpu.VMEM((order, order), f32),
             pltpu.VMEM((np_, depth, electrons), f32),
@@ -461,12 +571,13 @@
             dma((8, np_)),
             dma((20, chips * pieces)),
             dma((4, np_)),
+            dma((2 + cols // 128 + max(1, 2 * electrons // EBLOCK),)),
         ],
         compiler_params=pltpu.CompilerParams(
             collective_id=1, has_side_effects=True, vmem_limit_bytes=60 * 1024 * 1024
         ),
         name="middle",
-    )(waves, low, chirp, tables)
+    )(waves, trial, chirp, tables)
 
 
 def newton_schulz(scaled, identity):
@@ -526,26 +637,21 @@
     return jnp.stack([chirp_re * out_re - chirp_im * out_im, chirp_re * out_im + chirp_im * out_re])
 
 
+def launch_chirp(row_total, cols):
+    row_term = (np.arange(row_total) - row_total / 2.0) ** 2 / row_total
+    col_term = (np.arange(cols) - cols / 2.0) ** 2 / cols
+    angle = math.pi * 0.5 * (row_term[:, None] + col_term[None, :])
+    return np.stack([np.cos(angle), np.sin(angle)]).astype(np.float32)
+
+
 def shards(wavefronts, trial_modes):
-    electrons_dev, _, rows_dev, cols = wavefronts.shape
-    mode_count = trial_modes.shape[1]
-    order = 2 * mode_count
-    pixels = rows_dev * cols
-    groups = lax.axis_size("elec")
-    share = mode_count // groups
-    waves = wavefronts.reshape(electrons_dev, 2 * pixels)
-    low = trial_modes.astype(jnp.bfloat16).reshape(order, pixels)
-
+    rows_dev, cols = wavefronts.shape[2:]
+    share = trial_modes.shape[1] // lax.axis_size("elec")
     pix_count = lax.axis_size("pix")
     row_total = rows_dev * pix_count
-    row_pos = (lax.axis_index("pix") * rows_dev + jnp.arange(rows_dev, dtype=jnp.int32)).astype(
-        jnp.float32
-    )
-    chirp = jnp.stack(
-        chirp_phase(row_pos, jnp.arange(cols, dtype=jnp.float32), row_total, cols, 0.5)
-    )
+    chirp = jnp.asarray(launch_chirp(row_total, cols).reshape(2, pix_count, rows_dev, cols))
     tables = jnp.asarray(column_tables(cols, pix_count))
-    column_block = middle(waves, low, chirp, tables, mode_count).reshape(row_total, -1)
+    column_block = middle(wavefronts, trial_modes, chirp, tables).reshape(row_total, -1)
     width = cols // pix_count
     col_pos = (lax.axis_index("pix") * width + jnp.arange(width, dtype=jnp.int32)).astype(
         jnp.float32

time: 122 us -> 108 us (0.89)
  local copies, waits for them, and re-layouts: 16.9 us -> 0.33 us
  Pallas kernels: 98.1 us -> 104 us
  other arithmetic: 4.43 us -> 1.67 us
    unnamed x4 -> x2, local copies, waits for them, and re-layouts: 16.6 us -> 0.01 us
    pallas_call x1, Pallas kernels: 98.1 us -> 104 us  [middle(): pl.pallas_call(functools.partial(core_kernel, np_, ne, pieces, sub, elect...]
    convert_element_type x1 -> x0, other arithmetic: 1.87 us -> none  [shards(): low = trial_modes.astype(jnp.bfloat16).reshape(order, pixels)]
where the time goes in v1:
time: 108 us
  Pallas kernels  104 us (96%)
  matrix products  1.8 us (2%)
  other arithmetic  1.67 us (2%)
    pallas_call x1, Pallas kernels, middle(): pl.pallas_call(functools.partial(core_kernel, np_, ne, pieces, sub, elect...  104 us

profile of v1, /device:TPU:0, one launch (start us, length us, event | category | flops | bytes accessed | tf_op | source)
XLA Modules:
  0.0 108.1 jit_solution(16239567711218232701)
XLA Ops:
  0.0 0.0 copy-start
  0.0 104.2 %middle.1 = bf16[8,40,512]{2,1,0:T(8,128)(2,1)} custom-call(bf16[384,2,5,8,256]{4,3,2,1,0:T(8,128)(2,1)} %bitcast.15, f32[2560,256]{1,0:T(8,128)} %bitcast.16, f32[2,8,40,256]{3,2,1,0:T(8,128)} %constant.26.clone.chirp_hbm, bf16[2,512,512]{2,1,0:T(8,128)(2,1)} %constant.27.clone.table_hbm), custom_call_target="tpu_custom_call" | custom-call | tf_op jit(solution)/shard_map/middle/pallas_call | solution.py:536
  104.2 0.0 copy-done
  104.3 1.8 %fusion.2 = f32[1280,512]{1,0:T(8,128)S(1)} fusion(bf16[1280,320]{1,0:T(8,128)(2,1)S(1)} %copy-done, bf16[320,512]{1,0:T(8,128)(2,1)} %bitcast.19), kind=kOutput, calls=%fused_computation.11 | convolution fusion | flops 419430400 | bytes 3768320 | tf_op jit(solution)/shard_map/dot_general | solution.py:628
  106.1 0.3 slice_add_fusion
  106.3 0.1 slice_add_fusion.1
  106.4 0.2 copy.10
  106.6 0.2 copy.11
  106.8 0.3 fusion.1
  107.1 0.1 subtract_bitcast_fusion
  107.2 0.9 pad_maximum_fusion
  (2 shorter events, 0.0 us)
Async XLA Ops:
  0.0 104.3 %copy-start = (bf16[1280,320]{1,0:T(8,128)(2,1)S(1)}, bf16[1280,320]{1,0:T(8,128)(2,1)}, u32[]{:S(2)}) copy-start(bf16[1280,320]{1,0:T(8,128)(2,1)} %constant.28.clone) | copy-start | bytes 2457604

commit v2 on v1

--- a/solution.py
+++ b/solution.py
@@ -72,7 +72,7 @@
 
 def core_kernel(
     np_, ne, pieces, sub, electrons, modes, raw,
-    waves_hbm, trial_hbm, chirp_hbm, table_hbm,
+    waves_hbm, trial_hbm, table_hbm,
     out_ref,
     stage_ref, waves_ref, trial_ref, low_ref, chirp_ref, table_ref, pick_ref,
     applied_ref, turn_ref, part_ref, lines_ref, launch_ref, spec_ref, send_ref, rows_a, both_ref, cut_ref, emb_ref,
@@ -125,10 +125,16 @@
             wave_copy(step).start()
     else:
         wave_copy = load(waves_hbm, waves_ref, 2 + panels)
-    late_copies = [
-        load(chirp_hbm.at[:, me_p], chirp_ref, 0),
-        load(table_hbm, table_ref, 1),
-    ]
+    table_copy = load(table_hbm, table_ref, 1)
+    row_pos = (lax.broadcasted_iota(jnp.int32, (rows, 128), 0) + me_p * rows).astype(jnp.float32)
+    col_pos = lax.broadcasted_iota(jnp.int32, (8, cols), 1).astype(jnp.float32)
+    row_all = float(rows * np_)
+    row_angle = (math.pi * 0.5) * (row_pos - row_all / 2.0) ** 2 / row_all
+    col_angle = (math.pi * 0.5) * (col_pos - cols / 2.0) ** 2 / float(cols)
+    row_cos, row_sin = jnp.cos(row_angle)[:, 0:1], jnp.sin(row_angle)[:, 0:1]
+    col_cos, col_sin = jnp.cos(col_angle)[0:1], jnp.sin(col_angle)[0:1]
+    chirp_ref[0] = row_cos * col_cos - row_sin * col_sin
+    chirp_ref[1] = row_sin * col_cos + row_cos * col_sin
     for copy in trial_copies:
         copy.wait()
 
@@ -137,8 +143,7 @@
             [trial_ref[b, pl.ds(row, order, stride=rows), :] for b in range(panels)], axis=1
         ).astype(jnp.bfloat16)
         at = pl.ds(pl.multiple_of(row * cols, 128), cols)
-        low_ref[0, :, at] = fields
-        low_ref[1, :, at] = jnp.concatenate([-fields[modes:], fields[:modes]], axis=0)
+        low_ref[:, at] = fields
         return carry
 
     lax.fori_loop(0, rows, lower_modes, 0)
@@ -165,43 +170,31 @@
             block, half_of = step // 2, lax.rem(step, 2)
             base = pl.multiple_of(block * batch, batch)
 
-            def sort_band(band_of, carry):
+            for band_of in range(rows // band):
                 sorted_tiles = []
                 for t in range(batch // 32):
                     mixed = stage_ref[pl.ds(base + t * 32, 32), half_of, band_of]
                     sorted_tiles.append(
                         dot(pick_ref[...], mixed.reshape(tile, cols), NN).astype(jnp.bfloat16)
                     )
-                by_row = []
                 for r in range(band):
-                    row_wave = jnp.concatenate(
-                        [value[r * 32 : (r + 1) * 32] for value in sorted_tiles], axis=0
-                    )
-                    waves_ref[half_of * rows + band_of * band + r, pl.ds(base, batch), :] = row_wave
-                    by_row.append(row_wave)
-                fields = low_ref[
-                    half_of, :, pl.ds(pl.multiple_of(band_of * band * cols, 128), band * cols)
-                ]
-                rows_a[:, pl.ds(base, batch)] += dot(
-                    fields, jnp.concatenate(by_row, axis=1), NT
-                )
-                return carry
-
-            lax.fori_loop(0, rows // band, sort_band, 0)
+                    for t in range(batch // 32):
+                        waves_ref[
+                            half_of * rows + band_of * band + r, pl.ds(base + t * 32, 32), :
+                        ] = sorted_tiles[t][r * 32 : (r + 1) * 32]
             return carry
 
         lax.fori_loop(0, 2 * blocks, sort_block, 0)
     else:
         wave_copy.wait()
 
-        def opening(step, carry):
-            at = pl.ds(pl.multiple_of(step * sub, 128), sub)
-            correlate(low_ref[0, :, at], step * lines)
-            return carry
-
-        lax.fori_loop(0, rows // lines, opening, 0)
-    for copy in late_copies:
-        copy.wait()
+    def opening(step, carry):
+        at = pl.ds(pl.multiple_of(step * sub, 128), sub)
+        correlate(low_ref[:, at], step * lines)
+        return carry
+
+    lax.fori_loop(0, rows // lines, opening, 0)
+    table_copy.wait()
     for j in range(np_):
         part_ref[j] = rows_a[pl.ds(j * depth, depth), 0:electrons]
     pl.semaphore_wait(pltpu.get_barrier_semaphore(), greeted)
@@ -505,7 +498,7 @@
         copy.wait_send()
 
 
-def middle(waves, trial, chirp, tables):
+def middle(waves, trial, tables):
     np_ = lax.axis_size("pix")
     ne = lax.axis_size("elec")
     electrons, _, rows, cols = waves.shape
@@ -536,13 +529,13 @@
     return pl.pallas_call(
         functools.partial(core_kernel, np_, ne, pieces, sub, electrons, mode_count, raw),
         out_shape=jax.ShapeDtypeStruct((np_, rows, lanes), bf16),
-        in_specs=[hbm] * 4,
+        in_specs=[hbm] * 3,
         out_specs=vmem,
         scratch_shapes=[
             pltpu.VMEM(stage, bf16),
             pltpu.VMEM((2 * rows, electrons, cols), bf16),
             pltpu.VMEM((cols // 128, order * rows, 128), f32),
-            pltpu.VMEM((2, order, pixels), bf16),
+            pltpu.VMEM((order, pixels), bf16),
             pltpu.VMEM((2, rows, cols), f32),
             pltpu.VMEM(tables.shape, bf16),
             pltpu.VMEM((256, 256), bf16),
@@ -577,7 +570,7 @@
             collective_id=1, has_side_effects=True, vmem_limit_bytes=60 * 1024 * 1024
         ),
         name="middle",
-    )(waves, trial, chirp, tables)
+    )(waves, trial, tables)
 
 
 def newton_schulz(scaled, identity):
@@ -637,21 +630,13 @@
     return jnp.stack([chirp_re * out_re - chirp_im * out_im, chirp_re * out_im + chirp_im * out_re])
 
 
-def launch_chirp(row_total, cols):
-    row_term = (np.arange(row_total) - row_total / 2.0) ** 2 / row_total
-    col_term = (np.arange(cols) - cols / 2.0) ** 2 / cols
-    angle = math.pi * 0.5 * (row_term[:, None] + col_term[None, :])
-    return np.stack([np.cos(angle), np.sin(angle)]).astype(np.float32)
-
-
 def shards(wavefronts, trial_modes):
     rows_dev, cols = wavefronts.shape[2:]
     share = trial_modes.shape[1] // lax.axis_size("elec")
     pix_count = lax.axis_size("pix")
     row_total = rows_dev * pix_count
-    chirp = jnp.asarray(launch_chirp(row_total, cols).reshape(2, pix_count, rows_dev, cols))
     tables = jnp.asarray(column_tables(cols, pix_count))
-    column_block = middle(wavefronts, trial_modes, chirp, tables).reshape(row_total, -1)
+    column_block = middle(wavefronts, trial_modes, tables).reshape(row_total, -1)
     width = cols // pix_count
     col_pos = (lax.axis_index("pix") * width + jnp.arange(width, dtype=jnp.int32)).astype(
         jnp.float32

time: 108 us -> 104 us (0.963)
  Pallas kernels: 104 us -> 99.7 us
    pallas_call x1, Pallas kernels: 104 us -> 99.7 us  [middle(): pl.pallas_call(functools.partial(core_kernel, np_, ne, pieces, sub, elect...]
where the time goes in v2:
time: 104 us
  Pallas kernels  99.7 us (96%)
  matrix products  1.81 us (2%)
  other arithmetic  1.67 us (2%)
    pallas_call x1, Pallas kernels, middle(): pl.pallas_call(functools.partial(core_kernel, np_, ne, pieces, sub, elect...  99.7 us

profile of v2, /device:TPU:0, one launch (start us, length us, event | category | flops | bytes accessed | tf_op | source)
XLA Modules:
  0.0 103.6 jit_solution(3416846364285060041)
XLA Ops:
  0.0 0.0 copy-start
  0.0 99.7 %middle.1 = bf16[8,40,512]{2,1,0:T(8,128)(2,1)} custom-call(bf16[384,2,5,8,256]{4,3,2,1,0:T(8,128)(2,1)} %bitcast.15, f32[2560,256]{1,0:T(8,128)} %bitcast.16, bf16[2,512,512]{2,1,0:T(8,128)(2,1)} %constant.24.clone.table_hbm), custom_call_target="tpu_custom_call" | custom-call | tf_op jit(solution)/shard_map/middle/pallas_call | solution.py:529
  99.7 0.0 copy-done
  99.7 1.8 %fusion.2 = f32[1280,512]{1,0:T(8,128)S(1)} fusion(bf16[1280,320]{1,0:T(8,128)(2,1)S(1)} %copy-done, bf16[320,512]{1,0:T(8,128)(2,1)} %bitcast.19), kind=kOutput, calls=%fused_computation.11 | convolution fusion | flops 419430400 | bytes 3768320 | tf_op jit(solution)/shard_map/dot_general | solution.py:621
  101.5 0.3 slice_add_fusion
  101.8 0.1 slice_add_fusion.1
  101.9 0.2 copy.9
  102.1 0.2 copy.10
  102.3 0.3 fusion.1
  102.5 0.1 subtract_bitcast_fusion
  102.6 0.9 pad_maximum_fusion
  (2 shorter events, 0.0 us)
Async XLA Ops:
  0.0 99.7 %copy-start = (bf16[1280,320]{1,0:T(8,128)(2,1)S(1)}, bf16[1280,320]{1,0:T(8,128)(2,1)}, u32[]{:S(2)}) copy-start(bf16[1280,320]{1,0:T(8,128)(2,1)} %constant.25.clone) | copy-start | bytes 2457604

commit v3 on v2

--- a/solution.py
+++ b/solution.py
@@ -43,7 +43,7 @@
     return lax.dot_general(left, right, dims, preferred_element_type=jnp.float32)
 
 
-def scatter_gather(n, peers, x_ref, held, out_ref, send_a, recv_a, send_b, recv_b):
+def scatter_gather(n, peers, x_ref, held, out_ref, send_a, recv_a, send_b, recv_b, store):
     me = lax.axis_index("pix")
     started = []
     scatter = []
@@ -52,11 +52,11 @@
         copy = remote(x_ref.at[peer], held.at[d], send_a.at[d], recv_a.at[d], "pix", peer)
         copy.start()
         scatter.append(copy)
-    total = x_ref[me]
+    total = x_ref[me].astype(jnp.float32)
     for d in range(1, n):
         scatter[d - 1].wait_recv()
-        total = total + held[d]
-    out_ref[me] = total
+        total = total + held[d].astype(jnp.float32)
+    store(total)
     for d in range(1, n):
         copy = remote(
             out_ref.at[me], out_ref.at[me], send_b.at[d], recv_b.at[d], "pix", peers[d - 1]
@@ -196,18 +196,30 @@
     lax.fori_loop(0, rows // lines, opening, 0)
     table_copy.wait()
     for j in range(np_):
-        part_ref[j] = rows_a[pl.ds(j * depth, depth), 0:electrons]
+        part_ref[j] = rows_a[pl.ds(j * depth, depth), 0:electrons].astype(jnp.bfloat16)
     pl.semaphore_wait(pltpu.get_barrier_semaphore(), greeted)
+    def store_first(total):
+        total_a[me_p] = total.astype(jnp.bfloat16)
+
+    def store_split(ref, lead, block):
+        upper = block.astype(jnp.bfloat16)
+        ref[lead] = upper
+        ref[lead, :, electrons + order : electrons + 2 * order] = (
+            block[:, electrons : electrons + order]
+            - upper[:, electrons : electrons + order].astype(jnp.float32)
+        ).astype(jnp.bfloat16)
+
+    def store_second(total):
+        gram = total[:, electrons : electrons + order] + total[:, electrons + order : electrons + 2 * order]
+        rows_a[0:depth, 0:electrons] = total[:, 0:electrons]
+        rows_a[0:depth, electrons : electrons + order] = gram
+        store_split(total_b, me_p, rows_a[0:depth, :])
+
     started = scatter_gather(
-        np_, peers, part_ref, held_a, total_a, ps.at[0], ps.at[1], ps.at[2], ps.at[3]
+        np_, peers, part_ref, held_a, total_a, ps.at[0], ps.at[1], ps.at[2], ps.at[3], store_first
     )
     for j in range(np_):
-        rows_a[pl.ds(j * depth, depth), 0:electrons] = total_a[j]
-
-    def split_rows(value):
-        upper = value.astype(jnp.bfloat16)
-        both_ref[0:order, :] = upper
-        both_ref[order : 2 * order, :] = (value - upper.astype(jnp.float32)).astype(jnp.bfloat16)
+        rows_a[pl.ds(j * depth, depth), 0:electrons] = total_a[j].astype(jnp.float32)
 
     def part(ref, lead, piece):
         return ref.at[lead, :, pl.ds(piece * width, width)]
@@ -215,7 +227,7 @@
     def cut(piece):
         return pl.ds(piece * width, width)
 
-    def round_trip(turn, gathered, finish, beside):
+    def round_trip(turn, gathered, finish, beside, scale=None):
         sa, ra, sb, rb, sc, rc, sd, rd, se, re = [es.at[10 * turn + i] for i in range(10)]
         first, second = {}, {}
 
@@ -226,10 +238,10 @@
                 both = both_ref[...]
                 from_re = dot(both, wave(0, row, lines), NN)
                 from_im = dot(both, wave(1, row, lines), NN)
-                from_re = from_re[:order] + from_re[order:]
-                from_im = from_im[:order] + from_im[order:]
                 real = from_re[:modes] + from_im[modes:]
                 imag = from_re[modes:] - from_im[:modes]
+                if scale is not None:
+                    real, imag = real * scale, imag * scale
                 if chunk % 16 == 0:
                     whole = jnp.concatenate([real, imag], axis=0).astype(jnp.bfloat16)
                     for j in range(ne):
@@ -325,7 +337,7 @@
             )
         return cut_ref[...].astype(jnp.bfloat16)
 
-    split_rows(rows_a[:, 0:electrons])
+    both_ref[...] = rows_a[:, 0:electrons].astype(jnp.bfloat16)
     rows_a[...] = jnp.zeros_like(rows_a)
 
     def project_piece(piece):
@@ -340,20 +352,21 @@
 
     round_trip(0, first_ref, project_piece, lambda: None)
     for j in range(np_):
-        pay_ref[j] = rows_a[pl.ds(j * depth, depth), :]
+        store_split(pay_ref, j, rows_a[pl.ds(j * depth, depth), :])
     started += scatter_gather(
-        np_, peers, pay_ref, held_b, total_b, ps.at[4], ps.at[5], ps.at[6], ps.at[7]
+        np_, peers, pay_ref, held_b, total_b, ps.at[4], ps.at[5], ps.at[6], ps.at[7], store_second
     )
     for j in range(np_):
-        rows_a[pl.ds(j * depth, depth), :] = total_b[j]
+        rows_a[pl.ds(j * depth, depth), :] = total_b[j].astype(jnp.float32)
 
     row_id = lax.broadcasted_iota(jnp.int32, (order, order), 0)
     col_id = lax.broadcasted_iota(jnp.int32, (order, order), 1)
-    raw = rows_a[:, electrons : electrons + order]
+    raw = rows_a[:, electrons : electrons + order] + rows_a[:, electrons + order : electrons + 2 * order]
     trace = 2.0 * jnp.sum(
         jnp.sum(jnp.where(row_id == col_id, raw, 0.0), axis=1, keepdims=True), axis=0, keepdims=True
     )
-    split_rows(rows_a[:, 0:electrons] / jnp.sqrt(trace))
+    both_ref[...] = rows_a[:, 0:electrons].astype(jnp.bfloat16)
+    scale = 1.0 / jnp.sqrt(trace)
 
     def first_turn():
         gram_re = raw[:modes, :modes] + raw[modes:, modes:]
@@ -374,7 +387,7 @@
 
         emb2[0] = lax.fori_loop(0, width // sub, body, emb2[0])
 
-    round_trip(1, applied_ref, gram_piece, first_turn)
+    round_trip(1, applied_ref, gram_piece, first_turn, scale)
     raw2 = emb2[0]
     gram_re = raw2[:modes, :modes] + raw2[modes:, modes:]
     gram_im = raw2[:modes, modes:] - raw2[modes:, :modes]
@@ -519,7 +532,7 @@
     lines = next(size for size in (5, 4, 2, 1) if rows // pieces % size == 0)
     sub = lines * cols
     chips = ne // 2
-    wide = electrons + order + -order % 128
+    wide = electrons + 2 * order + -2 * order % 128
     share = mode_count // ne
     lanes = 2 * share * (cols // np_)
     vmem = pl.BlockSpec(memory_space=pltpu.VMEM)
@@ -541,20 +554,20 @@
             pltpu.VMEM((256, 256), bf16),
             pltpu.VMEM((ne, chunk, pixels), bf16),
             pltpu.VMEM((order, order), f32),
-            pltpu.VMEM((np_, depth, electrons), f32),
+            pltpu.VMEM((np_, depth, electrons), bf16),
             pltpu.VMEM((cols // 128, rows * 2 * share, 128), f32),
             pltpu.VMEM((share * rows, 2 * cols), f32),
             pltpu.VMEM((share * rows, 2 * cols), f32),
             pltpu.VMEM((np_, rows, lanes), bf16),
             pltpu.VMEM((order, wide), f32),
-            pltpu.VMEM((2 * order, electrons), bf16),
+            pltpu.VMEM((order, electrons), bf16),
             pltpu.VMEM((order, sub), f32),
             pltpu.VMEM((order, order), f32),
-            pltpu.VMEM((np_, depth, electrons), f32),
-            pltpu.VMEM((np_, depth, electrons), f32),
-            pltpu.VMEM((np_, depth, wide), f32),
-            pltpu.VMEM((np_, depth, wide), f32),
-            pltpu.VMEM((np_, depth, wide), f32),
+            pltpu.VMEM((np_, depth, electrons), bf16),
+            pltpu.VMEM((np_, depth, electrons), bf16),
+            pltpu.VMEM((np_, depth, wide), bf16),
+            pltpu.VMEM((np_, depth, wide), bf16),
+            pltpu.VMEM((np_, depth, wide), bf16),
             pltpu.VMEM((2, ne, chunk, pixels), bf16),
             pltpu.VMEM((2, chips, chunk, pixels), bf16),
             pltpu.VMEM((2, chips, chunk, pixels), bf16),

time: 104 us -> 103 us (level)
  Pallas kernels: 99.7 us -> 98.5 us
    pallas_call x1, Pallas kernels: 99.7 us -> 98.5 us  [middle(): pl.pallas_call(functools.partial(core_kernel, np_, ne, pieces, sub, elect...]
where the time goes in v3:
time: 103 us; the launch traced here: 102 us
  Pallas kernels  98.5 us (96%)
  matrix products  1.81 us (2%)
  other arithmetic  1.67 us (2%)
    pallas_call x1, Pallas kernels, middle(): pl.pallas_call(functools.partial(core_kernel, np_, ne, pieces, sub, elect...  98.5 us

profile of v3, /device:TPU:0, one launch (start us, length us, event | category | flops | bytes accessed | tf_op | source)
XLA Modules:
  0.0 102.4 jit_solution(3913578203572913482)
XLA Ops:
  0.0 0.0 copy-start
  0.0 98.5 %middle.1 = bf16[8,40,512]{2,1,0:T(8,128)(2,1)} custom-call(bf16[384,2,5,8,256]{4,3,2,1,0:T(8,128)(2,1)} %bitcast.15, f32[2560,256]{1,0:T(8,128)} %bitcast.16, bf16[2,512,512]{2,1,0:T(8,128)(2,1)} %constant.24.clone.table_hbm), custom_call_target="tpu_custom_call" | custom-call | tf_op jit(solution)/shard_map/middle/pallas_call | solution.py:542
  98.5 0.0 copy-done
  98.5 1.8 %fusion.2 = f32[1280,512]{1,0:T(8,128)S(1)} fusion(bf16[1280,320]{1,0:T(8,128)(2,1)S(1)} %copy-done, bf16[320,512]{1,0:T(8,128)(2,1)} %bitcast.19), kind=kOutput, calls=%fused_computation.11 | convolution fusion | flops 419430400 | bytes 3768320 | tf_op jit(solution)/shard_map/dot_general | solution.py:634
  100.3 0.3 slice_add_fusion
  100.6 0.1 slice_add_fusion.1
  100.7 0.2 copy.9
  100.9 0.2 copy.10
  101.1 0.3 fusion.1
  101.3 0.1 subtract_bitcast_fusion
  101.4 0.9 pad_maximum_fusion
  (2 shorter events, 0.0 us)
Async XLA Ops:
  0.0 98.5 %copy-start = (bf16[1280,320]{1,0:T(8,128)(2,1)S(1)}, bf16[1280,320]{1,0:T(8,128)(2,1)}, u32[]{:S(2)}) copy-start(bf16[1280,320]{1,0:T(8,128)(2,1)} %constant.25.clone) | copy-start | bytes 2457604

commit v4 on v3

--- a/solution.py
+++ b/solution.py
@@ -16,21 +16,20 @@
 EBLOCK = 128
 
 
-def greet(*groups):
+def greet(targets):
     barrier = pltpu.get_barrier_semaphore()
-    for axis, peers in groups:
-        for peer in peers:
-            pl.semaphore_signal(barrier, inc=1, device_id={axis: peer}, device_id_type=MESH)
-    return sum(len(peers) for _, peers in groups)
-
-
-def remote(src, dst, send_sem, recv_sem, axis, peer):
+    for target in targets:
+        pl.semaphore_signal(barrier, inc=1, device_id=target, device_id_type=MESH)
+    return len(targets)
+
+
+def remote(src, dst, send_sem, recv_sem, axis, peer=None):
     return pltpu.make_async_remote_copy(
         src_ref=src,
         dst_ref=dst,
         send_sem=send_sem,
         recv_sem=recv_sem,
-        device_id={axis: peer},
+        device_id=axis if peer is None else {axis: peer},
         device_id_type=MESH,
     )
 
@@ -71,14 +70,15 @@
 
 
 def core_kernel(
-    np_, ne, pieces, sub, electrons, modes, raw,
+    np_, ne, pieces, sub, electrons, modes, raw, bands,
     waves_hbm, trial_hbm, table_hbm,
     out_ref,
     stage_ref, waves_ref, trial_ref, low_ref, chirp_ref, table_ref, pick_ref,
     applied_ref, turn_ref, part_ref, lines_ref, launch_ref, spec_ref, send_ref, rows_a, both_ref, cut_ref, emb_ref,
     held_a, total_a, pay_ref, held_b, total_b,
     x_ref, pair, half, far, first_ref, gram_in,
-    ps, es, gs, load_sem,
+    x2_ref, pair2, half2, far2, own_ref, gram_e, panel_ref, send2_ref,
+    ps, es, gs, load_sem, ts, ge, fs,
 ):
     share = modes // ne
     rows, cols = chirp_ref.shape[1:]
@@ -98,7 +98,18 @@
     others = [lax.rem(chip + d, chips) for d in range(1, chips)]
     seats = [other * 2 + core for other in others]
     sources = [lax.rem(chip + chips - d, chips) for d in range(1, chips)]
-    greeted = greet(("pix", peers), ("elec", [partner] + seats))
+    if bands:
+        ring = [
+            (de, dp, {"elec": lax.rem(me + de, ne), "pix": lax.rem(me_p + dp, np_)})
+            for de in range(ne)
+            for dp in range(np_)
+            if de or dp
+        ]
+        greeted = greet([target for _, _, target in ring])
+    else:
+        greeted = greet(
+            [{"pix": peer} for peer in peers] + [{"elec": peer} for peer in [partner] + seats]
+        )
     rows_a[...] = jnp.zeros_like(rows_a)
 
     def load(src, dst, slot):
@@ -387,7 +398,78 @@
 
         emb2[0] = lax.fori_loop(0, width // sub, body, emb2[0])
 
-    round_trip(1, applied_ref, gram_piece, first_turn, scale)
+    def split_trip():
+        deep = rows // (bands * ne)
+        span = deep * cols
+        sa, ra, sb, rb = [ts.at[i] for i in range(4)]
+        first, second = {}, {}
+
+        def at(piece):
+            return pl.ds(piece * span, span)
+
+        def compute(piece):
+            def body(step, carry):
+                row = piece * ne * deep + step * 2 * deep
+                both = both_ref[...]
+                from_re = dot(both, wave(0, row, 2 * deep), NN)
+                from_im = dot(both, wave(1, row, 2 * deep), NN)
+                real = (from_re[:modes] + from_im[modes:]) * scale
+                imag = (from_re[modes:] - from_im[:modes]) * scale
+                whole = jnp.concatenate([real, imag], axis=0).astype(jnp.bfloat16)
+                for k in range(2):
+                    x2_ref[2 * step + k, :, at(piece)] = whole[:, k * span : (k + 1) * span]
+                return carry
+
+            lax.fori_loop(0, ne // 2, body, 0)
+            for d, other in enumerate(others + [chip]):
+                slot = d * bands + piece
+                copy = remote(
+                    x2_ref.at[other * 2 + 1 - core, :, at(piece)], pair2.at[d, :, at(piece)],
+                    sa.at[slot], ra.at[slot], "elec", partner,
+                )
+                copy.start()
+                started.append(copy)
+                first[d, piece] = copy
+
+        def cross(piece):
+            for d in range(chips - 1):
+                slot = d * bands + piece
+                first[d, piece].wait_recv()
+                half2[d, :, at(piece)] = (
+                    x2_ref[seats[d], :, at(piece)].astype(jnp.float32)
+                    + pair2[d, :, at(piece)].astype(jnp.float32)
+                ).astype(jnp.bfloat16)
+                copy = remote(
+                    half2.at[d, :, at(piece)], far2.at[d, :, at(piece)],
+                    sb.at[slot], rb.at[slot], "elec", seats[d],
+                )
+                copy.start()
+                started.append(copy)
+                second[d, piece] = copy
+
+        def close(piece):
+            first[chips - 1, piece].wait_recv()
+            total = x2_ref[me, :, at(piece)].astype(jnp.float32) + pair2[
+                chips - 1, :, at(piece)
+            ].astype(jnp.float32)
+            for d in range(chips - 1):
+                second[d, piece].wait_recv()
+                total = total + far2[d, :, at(piece)].astype(jnp.float32)
+            own_ref[:, at(piece)] = total
+            fields = total.astype(jnp.bfloat16)
+            emb2[0] = emb2[0] + dot(fields, fields, NT)
+
+        for tick in range(bands + 3):
+            for lag, stage in ((0, compute), (1, cross), (3, close)):
+                if 0 <= tick - lag < bands:
+                    stage(tick - lag)
+            if tick == bands:
+                first_turn()
+
+    if bands:
+        split_trip()
+    else:
+        round_trip(1, applied_ref, gram_piece, first_turn, scale)
     raw2 = emb2[0]
     gram_re = raw2[:modes, :modes] + raw2[modes:, modes:]
     gram_im = raw2[:modes, modes:] - raw2[modes:, :modes]
@@ -397,6 +479,20 @@
     gram_in[0, :, 0:order] = emb_ref[0:low, 0:order]
     gram_in[0, :, order : 2 * order] = emb_ref[low:modes, 0:order]
     last = []
+    if bands:
+        gram_e[0] = gram_in[0]
+        for d in range(1, ne):
+            copy = remote(
+                gram_e.at[0], gram_e.at[d], ge.at[0, d], ge.at[1, d], "elec", lax.rem(me + d, ne)
+            )
+            copy.start()
+            last.append(copy)
+        total = gram_e[0]
+        for d in range(1, ne):
+            last[d - 1].wait_recv()
+            total = total + gram_e[d]
+        gram_in[0] = total
+    met = len(last)
     for d in range(1, np_):
         copy = remote(
             gram_in.at[0], gram_in.at[d], gs.at[0, d], gs.at[1, d], "pix", peers[d - 1]
@@ -405,7 +501,7 @@
         last.append(copy)
     total = gram_in[0]
     for d in range(1, np_):
-        last[d - 1].wait_recv()
+        last[met + d - 1].wait_recv()
         total = total + gram_in[d]
     emb_ref[0:low, 0:order] = total[:, 0:order]
     emb_ref[low:modes, 0:order] = total[:, order : 2 * order]
@@ -433,6 +529,12 @@
     identity = jnp.where(diagonal, 1.0, 0.0).astype(jnp.float32)
     second_root = newton_schulz(embedded / trace, identity) / jnp.sqrt(trace)
     turn_ref[...] = jnp.dot(second_root.T, first_t, precision=HIGH)
+    if bands:
+        finish_split(
+            np_, ne, bands, modes, rows, cols, ring, me, me_p, turn_ref[...], own_ref, chirp_ref,
+            table_ref, launch_ref, panel_ref, send2_ref, out_ref, fs, started + last,
+        )
+        return
     for part_of in range(2):
         emb_ref[pl.ds(part_of * share, share), :] = turn_ref[
             pl.ds(part_of * modes + me * share, share), :
@@ -511,6 +613,66 @@
         copy.wait_send()
 
 
+def finish_split(
+    np_, ne, bands, modes, rows, cols, ring, me, me_p, turn, own_ref, chirp_ref,
+    table_ref, launch_ref, panel_ref, send2_ref, out_ref, fs, copies,
+):
+    deep = rows // (bands * ne)
+    held = bands * deep
+    share = modes // ne
+    upper = turn.astype(jnp.bfloat16)
+    lower = (turn - upper.astype(jnp.float32)).astype(jnp.bfloat16)
+    for line in range(held):
+        row = line // deep * ne * deep + me * deep + line % deep
+        fields = own_ref[:, line * cols : (line + 1) * cols]
+        big = fields.astype(jnp.bfloat16)
+        small = (fields - big.astype(jnp.float32)).astype(jnp.bfloat16)
+        turned = dot(upper, big, NN) + dot(lower, big, NN) + dot(upper, small, NN)
+        real, imag = turned[:modes], turned[modes:]
+        chirp_re = chirp_ref[0, pl.ds(row, 1), :]
+        chirp_im = chirp_ref[1, pl.ds(row, 1), :]
+        at = pl.ds(line * modes, modes)
+        launch_ref[at, 0:cols] = chirp_re * real - chirp_im * imag
+        launch_ref[at, cols : 2 * cols] = chirp_re * imag + chirp_im * real
+    launch = launch_ref[...]
+    big = launch.astype(jnp.bfloat16)
+    small = (launch - big.astype(jnp.float32)).astype(jnp.bfloat16)
+    spectrum = (
+        dot(big, table_ref[0], NN) + dot(big, table_ref[1], NN) + dot(small, table_ref[0], NN)
+    )
+    for b in range(2 * cols // 128):
+        panel_ref[b] = spectrum[:, b * 128 : (b + 1) * 128]
+    for b in range(2 * cols // 128):
+        for m in range(0, modes, 2):
+            left = panel_ref[b, pl.ds(m, held, stride=modes), :]
+            right = panel_ref[b, pl.ds(m + 1, held, stride=modes), :]
+            to = m % share * 64
+            for k in range(2):
+                send2_ref[m // share, 2 * b + k, :, to : to + 128] = jnp.concatenate(
+                    [left[:, k * 64 : k * 64 + 64], right[:, k * 64 : k * 64 + 64]], axis=1
+                ).astype(jnp.bfloat16)
+    swaps = []
+    for de, dp, target in ring:
+        copy = remote(
+            send2_ref.at[target["elec"], target["pix"]], out_ref.at[me_p, me],
+            fs.at[0, de, dp], fs.at[1, de, dp], target,
+        )
+        copy.start()
+        swaps.append(copy)
+    out_ref[me_p, me] = send2_ref[me, me_p]
+    for de, dp, target in ring:
+        block = out_ref.at[lax.rem(me_p + np_ - dp, np_), lax.rem(me + ne - de, ne)]
+        remote(block, block, fs.at[0, de, dp], fs.at[1, de, dp], target).wait_recv()
+    for copy in copies + swaps:
+        copy.wait_send()
+
+
+def band_count(rows, cols, np_, ne, modes):
+    if ne % 2 or 2 * cols // np_ != 64 or modes // ne % 2:
+        return 0
+    return next((count for count in (5, 4, 2, 1) if rows % (count * ne) == 0), 0)
+
+
 def middle(waves, trial, tables):
     np_ = lax.axis_size("pix")
     ne = lax.axis_size("elec")
@@ -535,13 +697,20 @@
     wide = electrons + 2 * order + -2 * order % 128
     share = mode_count // ne
     lanes = 2 * share * (cols // np_)
+    bands = band_count(rows, cols, np_, ne, mode_count)
+    turns = 1 if bands else 2
+    held = rows // ne if bands else 8
+    strip = held * cols
+    old = 128 if bands else pixels
+    spare = mode_count if bands else 8
+    shape = (np_, ne, held, lanes) if bands else (np_, rows, lanes)
     vmem = pl.BlockSpec(memory_space=pltpu.VMEM)
     hbm = pl.BlockSpec(memory_space=pl.ANY)
     dma = pltpu.SemaphoreType.DMA
     f32, bf16 = jnp.float32, jnp.bfloat16
     return pl.pallas_call(
-        functools.partial(core_kernel, np_, ne, pieces, sub, electrons, mode_count, raw),
-        out_shape=jax.ShapeDtypeStruct((np_, rows, lanes), bf16),
+        functools.partial(core_kernel, np_, ne, pieces, sub, electrons, mode_count, raw, bands),
+        out_shape=jax.ShapeDtypeStruct(shape, bf16),
         in_specs=[hbm] * 3,
         out_specs=vmem,
         scratch_shapes=[
@@ -552,7 +721,7 @@
             pltpu.VMEM((2, rows, cols), f32),
             pltpu.VMEM(tables.shape, bf16),
             pltpu.VMEM((256, 256), bf16),
-            pltpu.VMEM((ne, chunk, pixels), bf16),
+            pltpu.VMEM((ne, chunk, old), bf16),
             pltpu.VMEM((order, order), f32),
             pltpu.VMEM((np_, depth, electrons), bf16),
             pltpu.VMEM((cols // 128, rows * 2 * share, 128), f32),
@@ -568,16 +737,27 @@
             pltpu.VMEM((np_, depth, wide), bf16),
             pltpu.VMEM((np_, depth, wide), bf16),
             pltpu.VMEM((np_, depth, wide), bf16),
-            pltpu.VMEM((2, ne, chunk, pixels), bf16),
-            pltpu.VMEM((2, chips, chunk, pixels), bf16),
-            pltpu.VMEM((2, chips, chunk, pixels), bf16),
-            pltpu.VMEM((2, chips, chunk, pixels), bf16),
+            pltpu.VMEM((turns, ne, chunk, pixels), bf16),
+            pltpu.VMEM((turns, chips, chunk, pixels), bf16),
+            pltpu.VMEM((turns, chips, chunk, pixels), bf16),
+            pltpu.VMEM((turns, chips, chunk, pixels), bf16),
             pltpu.VMEM((ne, chunk, pixels), bf16),
             pltpu.VMEM((np_, mode_count // 2, 2 * order), f32),
+            pltpu.VMEM((ne, 2 * spare, strip), bf16),
+            pltpu.VMEM((chips, 2 * spare, strip), bf16),
+            pltpu.VMEM((chips, 2 * spare, strip), bf16),
+            pltpu.VMEM((chips, 2 * spare, strip), bf16),
+            pltpu.VMEM((2 * spare, strip), f32),
+            pltpu.VMEM((ne, mode_count // 2, 2 * order), f32),
+            pltpu.VMEM((2 * cols // 128, held * spare, 128), f32),
+            pltpu.VMEM((ne, np_, held, lanes), bf16),
             dma((8, np_)),
             dma((20, chips * pieces)),
             dma((4, np_)),
             dma((2 + cols // 128 + max(1, 2 * electrons // EBLOCK),)),
+            dma((4, chips * max(1, bands))),
+            dma((2, ne)),
+            dma((2, ne, np_)),
         ],
         compiler_params=pltpu.CompilerParams(
             collective_id=1, has_side_effects=True, vmem_limit_bytes=60 * 1024 * 1024
@@ -643,18 +823,46 @@
     return jnp.stack([chirp_re * out_re - chirp_im * out_im, chirp_re * out_im + chirp_im * out_re])
 
 
+def row_section_split(block, bands, share, col_pos, row_total, col_total):
+    np_, ne, held, _ = block.shape
+    deep = held // bands
+    j, i, line = np.meshgrid(np.arange(np_), np.arange(ne), np.arange(held), indexing="ij")
+    order = (j * held * ne + line // deep * ne * deep + i * deep + line % deep).reshape(-1)
+    width = col_pos.shape[0]
+    pad = -row_total % 128
+    table = np.pad(np.stack(dft_table(row_total))[:, :, order], ((0, 0), (0, pad), (0, 0)))
+    tables = jnp.asarray(np.concatenate(split(table.reshape(-1, row_total)), axis=0))
+    wide = lax.dot_general(
+        block.reshape(row_total, -1), tables, (((0,), (1,)), ((), ())),
+        preferred_element_type=jnp.float32,
+    )
+    full = row_total + pad
+    wide = wide[:, : 2 * full] + wide[:, 2 * full :]
+    wide = wide.reshape(share, 2, width, 2 * full)
+    first, second = wide[..., :row_total], wide[..., full : full + row_total]
+    out_re = first[:, 0] - second[:, 1]
+    out_im = second[:, 0] + first[:, 1]
+    row_pos = jnp.arange(row_total, dtype=jnp.float32)
+    chirp_re, chirp_im = chirp_phase(col_pos, row_pos, col_total, row_total, 0.25)
+    out = jnp.stack([chirp_re * out_re - chirp_im * out_im, chirp_re * out_im + chirp_im * out_re])
+    return out.transpose(0, 1, 3, 2)
+
+
 def shards(wavefronts, trial_modes):
     rows_dev, cols = wavefronts.shape[2:]
     share = trial_modes.shape[1] // lax.axis_size("elec")
     pix_count = lax.axis_size("pix")
     row_total = rows_dev * pix_count
     tables = jnp.asarray(column_tables(cols, pix_count))
-    column_block = middle(wavefronts, trial_modes, tables).reshape(row_total, -1)
+    column_block = middle(wavefronts, trial_modes, tables)
     width = cols // pix_count
     col_pos = (lax.axis_index("pix") * width + jnp.arange(width, dtype=jnp.int32)).astype(
         jnp.float32
     )
-    return row_section(column_block, share, col_pos, row_total, cols)
+    bands = band_count(rows_dev, cols, pix_count, lax.axis_size("elec"), trial_modes.shape[1])
+    if bands:
+        return row_section_split(column_block, bands, share, col_pos, row_total, cols)
+    return row_section(column_block.reshape(row_total, -1), share, col_pos, row_total, cols)
 
 
 def solution(mesh):

time: 103 us -> 102 us (level)
  Pallas kernels: 98.5 us -> 97.3 us
    reshape x0 -> x1, local copies, waits for them, and re-layouts: none -> 1.16 us  [row_section_split(): block.reshape(row_total, -1)]
    pallas_call x1, Pallas kernels: 98.5 us -> 97.3 us  [middle(): pl.pallas_call(functools.partial(core_kernel, np_, ne, pieces, sub, elect...]
    another operation x2 -> x0, other arithmetic: 1.04 us -> none  [row_section(): jnp.stack([chirp_re * out_re - chirp_im * out_im, chirp_re * out_im + chi...]
where the time goes in v4:
time: 102 us; the launch traced here: 101 us
  Pallas kernels  97.3 us (95%)
  other arithmetic  1.52 us (1%)
  local copies, waits for them, and re-layouts  1.17 us (1%)
  matrix products  1.04 us (1%)
    pallas_call x1, Pallas kernels, middle(): pl.pallas_call(functools.partial(core_kernel, np_, ne, pieces, sub, elect...  97.3 us

profile of v4, /device:TPU:0, one launch (start us, length us, event | category | flops | bytes accessed | tf_op | source)
XLA Modules:
  0.0 101.1 jit_solution(16833083988623335330)
XLA Ops:
  0.0 0.3 fusion.5
  0.3 0.0 copy-start
  0.3 97.3 %middle.1 = bf16[8,4,10,512]{3,2,1,0:T(8,128)(2,1)} custom-call(bf16[384,2,5,8,256]{4,3,2,1,0:T(8,128)(2,1)} %bitcast.55, f32[2560,256]{1,0:T(8,128)} %bitcast.57, bf16[2,512,512]{2,1,0:T(8,128)(2,1)} %constant.24.clone.table_hbm), custom_call_target="tpu_custom_call" | custom-call | tf_op jit(solution)/shard_map/middle/pallas_call | solution.py:711
  97.6 1.2 %reshape.154 = bf16[320,512]{1,0:T(8,128)(2,1)S(1)} reshape(bf16[8,4,10,512]{3,2,1,0:T(8,128)(2,1)} %middle.1) | data formatting | bytes 655360 | tf_op jit(solution)/shard_map/reshape | solution.py:836
  98.8 0.0 copy-done
  98.8 1.0 %fusion.6 = f32[512,1536]{1,0:T(8,128)S(1)} fusion(bf16[320,512]{1,0:T(8,128)(2,1)S(1)} %reshape.154, bf16[1536,320]{1,0:T(8,128)(2,1)S(1)} %copy-done), kind=kOutput, calls=%fused_computation.17 | convolution fusion | flops 503316480 | bytes 4456448 | tf_op jit(solution)/shard_map/dot_general | solution.py:835
  99.8 0.2 slice_add_fusion
  100.0 0.1 multiply_subtract_fusion
  100.2 0.9 maximum_bitcast_fusion
  (2 shorter events, 0.0 us)
Async XLA Ops:
  0.3 98.5 %copy-start = (bf16[1536,320]{1,0:T(8,128)(2,1)S(1)}, bf16[1536,320]{1,0:T(8,128)(2,1)}, u32[]{:S(2)}) copy-start(bf16[1536,320]{1,0:T(8,128)(2,1)} %constant.25.clone) | copy-start | bytes 2949124
